TPU v7x, 256 devices: a whole 4x4x8 slice. The times are simulated.
256 devices in a mesh: wide: 32 (over z, y_lo, core), narrow: 8 (over x, y_hi).
Axes of the slice: x: 4, y: 4 (y_hi: 2, y_lo: 2; y = y_hi * 2 + y_lo), z: 8, core: 2. Of those that a mesh axis runs over, the one named last changes fastest.
Arguments:
- gradient: bfloat16 [40960, 16384], P(('wide', 'narrow')), may hold values from -81 to 81
- seating: int32 [64], replicated, may hold values from 0 to 63, each once
Outputs:
- rotated: bfloat16 [40960, 16384], P(('wide', 'narrow'))
Inputs may be any that keep to these rules, and one draw needn't show every extreme that they name: `seating`: each of the 64 block numbers is the seat of exactly one block.
All inputs are finite; a program needn't handle non-finite values.
Results may differ from a plain program's by a relative error of at most 0.0075.
Values may be sent and summed in bfloat16 or wider, within the bound.
A program may use at most 64 MiB of HBM per device.

v0:
```python
import jax
import jax.numpy as jnp
from jax import lax
from jax.sharding import PartitionSpec as P

ROUNDS = 8
STEPS = 2


def advance(seat_of, total_slots):
    pair_count = total_slots // 2
    cycle_pos = jnp.where(seat_of % 2 == 0, seat_of // 2 - 1, total_slots - 2 - (seat_of - 1) // 2)
    next_pos = (cycle_pos + 1) % (total_slots - 1)
    new_slot = jnp.where(
        next_pos < pair_count - 1, 2 * (next_pos + 1), 2 * (total_slots - 2 - next_pos) + 1
    )
    return jnp.where(seat_of == 0, 0, new_slot)


def occupants(seat_of, total_slots):
    block_ids = jnp.arange(total_slots, dtype=jnp.int32)
    matches = seat_of[None, :] == block_ids[:, None]
    return jnp.sum(jnp.where(matches, block_ids[None, :], 0), axis=1)


def rotate_columns(matrix, cosine, sine_part):
    width = cosine.shape[0]
    left_cols = matrix[:, :width]
    right_cols = matrix[:, width:]
    return jnp.concatenate(
        [left_cols * cosine - right_cols * sine_part, left_cols * sine_part + right_cols * cosine],
        axis=1,
    )


def roll_second(matrix, offset, which_axis):
    head_part, tail_part = jnp.split(matrix, 2, axis=which_axis)
    return jnp.concatenate(
        [head_part, jnp.roll(tail_part, offset, axis=which_axis)], axis=which_axis
    )


def one_round(round_index, carried):
    gram_mat, rotation = carried
    width = gram_mat.shape[0] // 2
    left_diag = jnp.diagonal(gram_mat[:width, :width])
    right_diag = jnp.diagonal(gram_mat[width:, width:])
    off_diag = jnp.diagonal(gram_mat[:width, width:])
    spread = right_diag - left_diag
    damping = (left_diag + right_diag) / 16.0 + 1e-06
    radius = jnp.sqrt(spread * spread + 4.0 * off_diag * off_diag + damping * damping)
    tangent = 2.0 * off_diag / (spread + radius)
    cosine = 1.0 / jnp.sqrt(1.0 + tangent * tangent)
    sine_part = tangent * cosine
    gram_mat = rotate_columns(gram_mat, cosine, sine_part)
    gram_mat = rotate_columns(gram_mat.T, cosine, sine_part).T
    rotation = rotate_columns(rotation, cosine, sine_part)
    gram_mat = roll_second(roll_second(gram_mat, -1, 0), -1, 1)
    rotation = roll_second(rotation, -1, 1)
    return (gram_mat, rotation)


def rotations(gram_mat):
    initial = (gram_mat, jnp.eye(gram_mat.shape[0], dtype=jnp.float32))
    gram_mat, rotation = lax.fori_loop(0, ROUNDS, one_round, initial)
    return roll_second(rotation, ROUNDS, 1)


def update_pair(paired):
    contract_dims = (((0,), (0,)), ((), ()))
    partial_gram = lax.dot_general(
        paired, paired, contract_dims, preferred_element_type=jnp.float32
    )
    gram_mat = lax.psum(partial_gram, "narrow")
    rotation = rotations(gram_mat).astype(jnp.bfloat16)
    return jnp.dot(paired, rotation, preferred_element_type=jnp.float32).astype(jnp.bfloat16)


def per_device(gradient, seating):
    count_wide = lax.axis_size("wide")
    row_count = gradient.shape[0]
    total_slots = 2 * count_wide
    block_width = gradient.shape[1] // total_slots
    seat_of = seating
    holders = occupants(seat_of, total_slots)
    seated = jnp.take(gradient.reshape(row_count, total_slots, block_width), holders, axis=1)
    seated = seated.reshape(row_count, count_wide, 2, block_width)
    arrived = lax.all_to_all(seated, "wide", split_axis=1, concat_axis=0, tiled=True)
    paired = arrived.reshape(count_wide * row_count, 2 * block_width)
    for section_index in range(STEPS):
        paired = update_pair(paired)
        if section_index + 1 < STEPS:
            following = advance(seat_of, total_slots)
            returned = lax.all_to_all(
                paired.reshape(count_wide * row_count, 1, 2, block_width),
                "wide",
                split_axis=0,
                concat_axis=1,
                tiled=True,
            )
            slotted = returned.reshape(row_count, total_slots, block_width)
            source_slots = jnp.take(seat_of, occupants(following, total_slots))
            regrouped = jnp.take(slotted, source_slots, axis=1).reshape(
                row_count, count_wide, 2, block_width
            )
            arrived = lax.all_to_all(regrouped, "wide", split_axis=1, concat_axis=0, tiled=True)
            paired = arrived.reshape(count_wide * row_count, 2 * block_width)
            seat_of = following
    returned = lax.all_to_all(
        paired.reshape(count_wide * row_count, 1, 2, block_width),
        "wide",
        split_axis=0,
        concat_axis=1,
        tiled=True,
    )
    slotted = returned.reshape(row_count, total_slots, block_width)
    return jnp.take(slotted, seat_of, axis=1).reshape(row_count, total_slots * block_width)


def solution(mesh):
    in_specs = (P(("wide", "narrow"), None), P())
    out_specs = P(("wide", "narrow"), None)
    return jax.shard_map(
        per_device, mesh=mesh, in_specs=in_specs, out_specs=out_specs, check_vma=False
    )
```

profile of v0, /device:TPU:1, one launch (start us, length us, event | category | flops | bytes accessed | tf_op | source)
XLA Modules:
  0.0 1019.4 jit_solution(16833773583891870454)
XLA Ops:
  7.3 5.5 copy.84
  12.9 5.7 gather_fusion.7
  18.6 5.4 broadcast_select_fusion.1
  23.9 10.2 copy.68
  34.1 129.0 %all_to_all.60 = bf16[160,32,2,256]{3,2,0,1:T(2,128)(2,1)S(1)} all-to-all(bf16[160,32,2,256]{3,2,0,1:T(2,128)(2,1)} %copy.68), channel_id=1, replica_groups=mesh['wide'=32,'narrow'=8] {'wide'}, dimensions={1} | all-to-all | bytes 10485760 | tf_op jit(solution)/shard_map/all_to_all | solution.py:88
  164.0 2.3 copy-done.3
  166.3 3.9 fusion.32
  171.4 85.2 %all-reduce.3.cloned.1.call-done = f32[512,512]{1,0:T(8,128)} async-done(((f32[512,512]{1,0:T(8,128)}), f32[512,512]{1,0:T(8,128)}) %all-reduce.3.cloned.1.call-update) | async-done | bytes 1048592 | tf_op jit(solution)/shard_map/psum | solution.py:74
  256.6 103.8 %while.24 = (s32[]{:T(128)}, f32[512,512]{1,0:T(8,128)}, f32[512,512]{0,1:T(8,128)}, s32[]{:T(128)}) while((s32[]{:T(128)}, f32[512,512]{1,0:T(8,128)}, f32[512,512]{0,1:T(8,128)}, s32[]{:T(128)}) %tuple.72), condition=%wide.region_3.5_spmd, body=%wide.region_2.4_spmd.sunk | while | flops 6034946 | bytes 28854352 | solution.py:65
  361.7 7.6 convolution_convert_fusion.1
  369.3 13.6 %copy.69 = bf16[5120,1,2,256]{3,2,1,0:T(2,128)(2,1)} copy(bf16[5120,1,2,256]{0,3,2,1:T(8,128)(2,1)} %bitcast.90) | data formatting | bytes 10485760 | tf_op jit(solution)/shard_map/reshape | solution.py:95
  382.9 12.9 %all-to-all-start.1 = ((bf16[5120,1,2,256]{3,2,1,0:T(2,128)(2,1)}), bf16[5120,1,2,256]{3,2,1,0:T(2,128)(2,1)}, u32[]{:S(2)}, u32[]{:S(2)}) async-start(bf16[5120,1,2,256]{3,2,1,0:T(2,128)(2,1)} %copy.69), calls=%async_computation.1 | async-start | bytes 10485760 | tf_op jit(solution)/shard_map/all_to_all | solution.py:94
  397.1 117.8 %all-to-all-done.1 = bf16[5120,1,2,256]{3,2,1,0:T(2,128)(2,1)} async-done(((bf16[5120,1,2,256]{3,2,1,0:T(2,128)(2,1)}), bf16[5120,1,2,256]{3,2,1,0:T(2,128)(2,1)}, u32[]{:S(2)}, u32[]{:S(2)}) %all-to-all-start.1) | async-done | bytes 5242912 | tf_op jit(solution)/shard_map/all_to_all | solution.py:94
  514.9 3.2 copy.70
  518.0 2.8 copy.71
  520.9 5.7 gather_fusion.8
  526.5 5.4 broadcast_select_fusion
  531.9 10.2 copy.72
  542.1 121.9 %all_to_all.61 = bf16[160,32,2,256]{3,2,0,1:T(2,128)(2,1)S(1)} all-to-all(bf16[160,32,2,256]{3,2,0,1:T(2,128)(2,1)} %copy.72), channel_id=1, replica_groups=mesh['wide'=32,'narrow'=8] {'wide'}, dimensions={1} | all-to-all | bytes 10485760 | tf_op jit(solution)/shard_map/all_to_all | solution.py:106
  664.9 2.3 copy-done.4
  667.2 3.9 fusion.33
  671.1 84.2 %all-reduce.5.cloned.1.call-done = f32[512,512]{1,0:T(8,128)} async-done(((f32[512,512]{1,0:T(8,128)}), f32[512,512]{1,0:T(8,128)}) %all-reduce.5.cloned.1.call-update) | async-done | bytes 1048592 | tf_op jit(solution)/shard_map/psum | solution.py:74
  755.3 86.5 %while.25 = (s32[]{:T(128)}, f32[512,512]{1,0:T(8,128)}, f32[512,512]{0,1:T(8,128)S(1)}, s32[]{:T(128)}) while((s32[]{:T(128)}, f32[512,512]{1,0:T(8,128)}, f32[512,512]{0,1:T(8,128)S(1)}, s32[]{:T(128)}) %tuple.75), condition=%wide.region_7.9_spmd, body=%wide.region_6.8_spmd.sunk | while | flops 6034946 | bytes 28854352 | solution.py:65
  842.0 7.6 convolution_convert_fusion
  849.5 13.6 %copy.73 = bf16[5120,1,2,256]{3,2,1,0:T(2,128)(2,1)} copy(bf16[5120,1,2,256]{0,3,2,1:T(8,128)(2,1)} %bitcast.91) | data formatting | bytes 10485760 | tf_op jit(solution)/shard_map/reshape | solution.py:110
  863.1 12.8 %all-to-all-start.3 = ((bf16[5120,1,2,256]{3,2,1,0:T(2,128)(2,1)}), bf16[5120,1,2,256]{3,2,1,0:T(2,128)(2,1)}, u32[]{:S(2)}, u32[]{:S(2)}) async-start(bf16[5120,1,2,256]{3,2,1,0:T(2,128)(2,1)} %copy.73), calls=%async_computation.3 | async-start | bytes 10485760 | tf_op jit(solution)/shard_map/all_to_all | solution.py:109
  875.9 119.0 %all-to-all-done.3 = bf16[5120,1,2,256]{3,2,1,0:T(2,128)(2,1)} async-done(((bf16[5120,1,2,256]{3,2,1,0:T(2,128)(2,1)}), bf16[5120,1,2,256]{3,2,1,0:T(2,128)(2,1)}, u32[]{:S(2)}, u32[]{:S(2)}) %all-to-all-start.3) | async-done | bytes 5242912 | tf_op jit(solution)/shard_map/all_to_all | solution.py:109
  995.0 3.2 copy.74
  998.2 2.8 copy.75
  1001.0 5.7 gather_fusion.9
  1006.6 3.0 select_bitcast_fusion
  1009.7 2.9 copy.80
  (385 shorter events, 194.4 us)
Async XLA Ops:
  6.5 250.1 %all-reduce.3.cloned.1.call-start = ((), (), s32[]{:S(2)}) async-start(), calls=%async_computation.4 | async-start | bytes 2097152 | tf_op jit(solution)/shard_map/psum | solution.py:74
  164.0 2.4 copy-start.3
  256.6 8.4 copy-start.1
  269.6 8.4 copy-start.1
  282.5 8.4 copy-start.1
  295.5 8.4 copy-start.1
  308.5 8.4 copy-start.1
  321.4 8.4 copy-start.1
  334.4 8.4 copy-start.1
  347.4 8.4 copy-start.1
  382.9 13.2 %copy-start = (s32[64]{0:T(128)S(1)}, s32[64]{0:T(128)}, u32[]{:S(2)}) copy-start(s32[64]{0:T(128)} %param.9) | copy-start | bytes 772
  382.9 132.0 %all-to-all-start.1 = ((bf16[5120,1,2,256]{3,2,1,0:T(2,128)(2,1)}), bf16[5120,1,2,256]{3,2,1,0:T(2,128)(2,1)}, u32[]{:S(2)}, u32[]{:S(2)}) async-start(bf16[5120,1,2,256]{3,2,1,0:T(2,128)(2,1)} %copy.69), calls=%async_computation.1 | async-start | bytes 10485760 | tf_op jit(solution)/shard_map/all_to_all | solution.py:94
  395.8 359.5 %all-reduce.5.cloned.1.call-start = ((), (), s32[]{:S(2)}) async-start(), calls=%async_computation.5 | async-start | bytes 2097152 | tf_op jit(solution)/shard_map/psum | solution.py:74
  664.9 2.4 copy-start.4
  755.3 8.4 copy-start.2
  766.1 8.4 copy-start.2
  776.9 8.4 copy-start.2
  787.7 8.4 copy-start.2
  798.6 8.4 copy-start.2
  809.4 8.4 copy-start.2
  820.2 8.4 copy-start.2
  831.0 8.4 copy-start.2
  863.1 131.8 %all-to-all-start.3 = ((bf16[5120,1,2,256]{3,2,1,0:T(2,128)(2,1)}), bf16[5120,1,2,256]{3,2,1,0:T(2,128)(2,1)}, u32[]{:S(2)}, u32[]{:S(2)}) async-start(bf16[5120,1,2,256]{3,2,1,0:T(2,128)(2,1)} %copy.73), calls=%async_computation.3 | async-start | bytes 10485760 | tf_op jit(solution)/shard_map/all_to_all | solution.py:109
Sparse Core Ops, SparseCore 0:
  170.4 86.1 all-reduce.2
  671.3 83.9 all-reduce.4
where the time goes:
time: 1020 us
  waiting for transfers between devices  406 us (40%)
  blocking collectives  251 us (25%)
  local copies, waits for them, and re-layouts  232 us (23%)
  other arithmetic  65.9 us (6%)
  starting transfers between devices  25.9 us (3%)
  matrix products  22.9 us (2%)
  between operations  13.6 us (1%)
    all_to_all x2, waiting for transfers between devices, per_device(): lax.all_to_all(paired.reshape(count_wide * row_count, 1, 2, block_width),...  237 us
    psum x2, waiting for transfers between devices, update_pair(): gram_mat = lax.psum(partial_gram, 'narrow')  169 us
    all_to_all x1, blocking collectives, per_device(): lax.all_to_all(seated, 'wide', split_axis=1, concat_axis=0, tiled=True)  129 us
    all_to_all x1, blocking collectives, per_device(): lax.all_to_all(regrouped, 'wide', split_axis=1, concat_axis=0, tiled=True)  122 us
    gather x16, local copies, waits for them, and re-layouts, one_round(): off_diag = jnp.diagonal(gram_mat[:width, width:])  37.5 us
    gather x16, local copies, waits for them, and re-layouts, one_round(): right_diag = jnp.diagonal(gram_mat[width:, width:])  37.5 us
    gather x16, local copies, waits for them, and re-layouts, one_round(): left_diag = jnp.diagonal(gram_mat[:width, :width])  37.5 us
    reshape x2, local copies, waits for them, and re-layouts, per_device(): paired.reshape(count_wide * row_count, 1, 2, block_width)  27.2 us
  transfers between devices with their start and end apart: 4, of which 4 were waited for; matrix products, arithmetic and copies ran while one was open for 0% of the time, Pallas kernels for 0%

commit v1 on v0

--- a/solution.py
+++ b/solution.py
@@ -71,7 +71,8 @@
     partial_gram = lax.dot_general(
         paired, paired, contract_dims, preferred_element_type=jnp.float32
     )
-    gram_mat = lax.psum(partial_gram, "narrow")
+    parts = lax.all_gather(partial_gram, "narrow", axis=0, tiled=False)
+    gram_mat = parts.sum(axis=0)
     rotation = rotations(gram_mat).astype(jnp.bfloat16)
     return jnp.dot(paired, rotation, preferred_element_type=jnp.float32).astype(jnp.bfloat16)
 

time: 1020 us -> 1040 us (1.020)
  waiting for transfers between devices: 406 us -> 455 us
  local copies, waits for them, and re-layouts: 232 us -> 213 us
    all_gather x0 -> x2, waiting for transfers between devices: none -> 218 us  [update_pair(): parts = lax.all_gather(partial_gram, 'narrow', axis=0, tiled=False)]
    psum x2 -> x0, waiting for transfers between devices: 169 us -> none  [update_pair(): gram_mat = lax.psum(partial_gram, 'narrow')]
    slice x16, local copies, waits for them, and re-layouts: 20 us -> 0.93 us  [one_round(): off_diag = jnp.diagonal(gram_mat[:width, width:])]
    concatenate x32, other arithmetic: 19.7 us -> 3.96 us  [roll_second(): jnp.concatenate([head_part, jnp.roll(tail_part, offset, axis=which_axis)]...]
where the time goes in v1:
time: 1040 us
  waiting for transfers between devices  455 us (44%)
  blocking collectives  252 us (24%)
  local copies, waits for them, and re-layouts  213 us (20%)
  other arithmetic  59.7 us (6%)
  matrix products  23 us (2%)
  starting transfers between devices  17 us (2%)
  between operations  13.9 us (1%)
    all_to_all x2, waiting for transfers between devices, per_device(): lax.all_to_all(paired.reshape(count_wide * row_count, 1, 2, block_width),...  237 us
    all_gather x2, waiting for transfers between devices, update_pair(): parts = lax.all_gather(partial_gram, 'narrow', axis=0, tiled=False)  218 us
    all_to_all x1, blocking collectives, per_device(): lax.all_to_all(seated, 'wide', split_axis=1, concat_axis=0, tiled=True)  130 us
    all_to_all x1, blocking collectives, per_device(): lax.all_to_all(regrouped, 'wide', split_axis=1, concat_axis=0, tiled=True)  122 us
    gather x16, local copies, waits for them, and re-layouts, one_round(): left_diag = jnp.diagonal(gram_mat[:width, :width])  37.5 us
    gather x16, local copies, waits for them, and re-layouts, one_round(): off_diag = jnp.diagonal(gram_mat[:width, width:])  37.5 us
    gather x16, local copies, waits for them, and re-layouts, one_round(): right_diag = jnp.diagonal(gram_mat[width:, width:])  37.5 us
    reshape x2, local copies, waits for them, and re-layouts, per_device(): paired.reshape(count_wide * row_count, 1, 2, block_width)  27.2 us
  transfers between devices with their start and end apart: 4, of which 4 were waited for; matrix products, arithmetic and copies ran while one was open for 0% of the time, Pallas kernels for 0%

profile of v1, /device:TPU:1, one launch (start us, length us, event | category | flops | bytes accessed | tf_op | source)
XLA Modules:
  0.0 1036.0 jit_solution(5412475428645500194)
XLA Ops:
  7.3 5.5 copy.84
  12.9 5.7 gather_fusion.7
  18.6 5.4 broadcast_select_fusion.1
  23.9 10.2 copy.68
  34.1 129.6 %all_to_all.60 = bf16[160,32,2,256]{3,2,0,1:T(2,128)(2,1)S(1)} all-to-all(bf16[160,32,2,256]{3,2,0,1:T(2,128)(2,1)} %copy.68), channel_id=1, replica_groups=mesh['wide'=32,'narrow'=8] {'wide'}, dimensions={1} | all-to-all | bytes 10485760 | tf_op jit(solution)/shard_map/all_to_all | solution.py:89
  167.0 3.9 fusion.32
  172.1 109.7 %all-gather.5.cloned.1.call-done = f32[4096,512]{1,0:T(8,128)} async-done(((f32[512,512]{1,0:T(8,128)}), f32[4096,512]{1,0:T(8,128)}) %all-gather.5.cloned.1.call-update) | async-done | bytes 8388624 | tf_op jit(solution)/shard_map/all_gather | solution.py:74
  281.7 4.5 reduce_sum.39
  286.2 87.0 %while.24 = (s32[]{:T(128)}, f32[512,512]{1,0:T(8,128)S(1)}, f32[512,512]{0,1:T(8,128)}, s32[]{:T(128)}) while((s32[]{:T(128)}, f32[512,512]{1,0:T(8,128)S(1)}, f32[512,512]{0,1:T(8,128)}, s32[]{:T(128)}) %tuple.72), condition=%wide.region_3.5_spmd, body=%wide.region_2.4_spmd.sunk | while | flops 6034946 | bytes 24660020 | solution.py:65
  374.6 7.6 convolution_convert_fusion.1
  382.2 13.6 %copy.69 = bf16[5120,1,2,256]{3,2,1,0:T(2,128)(2,1)} copy(bf16[5120,1,2,256]{0,3,2,1:T(8,128)(2,1)} %bitcast.94) | data formatting | bytes 10485760 | tf_op jit(solution)/shard_map/reshape | solution.py:96
  395.8 8.5 all-to-all-start.1
  405.5 117.9 %all-to-all-done.1 = bf16[5120,1,2,256]{3,2,1,0:T(2,128)(2,1)} async-done(((bf16[5120,1,2,256]{3,2,1,0:T(2,128)(2,1)}), bf16[5120,1,2,256]{3,2,1,0:T(2,128)(2,1)}, u32[]{:S(2)}, u32[]{:S(2)}) %all-to-all-start.1) | async-done | bytes 5242912 | tf_op jit(solution)/shard_map/all_to_all | solution.py:95
  523.3 3.2 copy.70
  526.5 2.8 copy.71
  529.3 5.7 gather_fusion.8
  535.0 5.4 broadcast_select_fusion
  540.4 10.2 copy.72
  550.6 122.4 %all_to_all.61 = bf16[160,32,2,256]{3,2,0,1:T(2,128)(2,1)S(1)} all-to-all(bf16[160,32,2,256]{3,2,0,1:T(2,128)(2,1)} %copy.72), channel_id=1, replica_groups=mesh['wide'=32,'narrow'=8] {'wide'}, dimensions={1} | all-to-all | bytes 10485760 | tf_op jit(solution)/shard_map/all_to_all | solution.py:107
  676.2 4.0 fusion.33
  680.2 108.5 %all-gather.7.cloned.1.call-done = f32[4096,512]{1,0:T(8,128)} async-done(((f32[512,512]{1,0:T(8,128)}), f32[4096,512]{1,0:T(8,128)}) %all-gather.7.cloned.1.call-update) | async-done | bytes 8388624 | tf_op jit(solution)/shard_map/all_gather | solution.py:74
  788.7 4.5 reduce_sum.42
  793.2 69.3 %while.25 = (s32[]{:T(128)}, f32[512,512]{1,0:T(8,128)S(1)}, f32[512,512]{0,1:T(8,128)S(1)}, s32[]{:T(128)}) while((s32[]{:T(128)}, f32[512,512]{1,0:T(8,128)S(1)}, f32[512,512]{0,1:T(8,128)S(1)}, s32[]{:T(128)}) %tuple.75), condition=%wide.region_7.9_spmd, body=%wide.region_6.8_spmd.sunk | while | flops 6034946 | bytes 24660020 | solution.py:65
  862.7 7.6 convolution_convert_fusion
  870.3 13.6 %copy.73 = bf16[5120,1,2,256]{3,2,1,0:T(2,128)(2,1)} copy(bf16[5120,1,2,256]{0,3,2,1:T(8,128)(2,1)} %bitcast.95) | data formatting | bytes 10485760 | tf_op jit(solution)/shard_map/reshape | solution.py:111
  883.9 8.3 all-to-all-start.3
  892.2 119.0 %all-to-all-done.3 = bf16[5120,1,2,256]{3,2,1,0:T(2,128)(2,1)} async-done(((bf16[5120,1,2,256]{3,2,1,0:T(2,128)(2,1)}), bf16[5120,1,2,256]{3,2,1,0:T(2,128)(2,1)}, u32[]{:S(2)}, u32[]{:S(2)}) %all-to-all-start.3) | async-done | bytes 5242912 | tf_op jit(solution)/shard_map/all_to_all | solution.py:110
  1011.3 3.2 copy.74
  1014.4 2.8 copy.75
  1017.3 5.7 gather_fusion.9
  1022.9 3.0 select_bitcast_fusion
  1026.0 2.9 copy.80
  (355 shorter events, 164.9 us)
Async XLA Ops:
  6.5 275.2 %all-gather.5.cloned.1.call-start = ((), (), s32[]{:S(2)}) async-start(), calls=%async_computation.4 | async-start | bytes 9437184 | tf_op jit(solution)/shard_map/all_gather | solution.py:74
  164.6 2.4 copy-start.1
  395.8 8.7 copy-start
  395.8 127.5 %all-to-all-start.1 = ((bf16[5120,1,2,256]{3,2,1,0:T(2,128)(2,1)}), bf16[5120,1,2,256]{3,2,1,0:T(2,128)(2,1)}, u32[]{:S(2)}, u32[]{:S(2)}) async-start(bf16[5120,1,2,256]{3,2,1,0:T(2,128)(2,1)} %copy.69), calls=%async_computation.1 | async-start | bytes 10485760 | tf_op jit(solution)/shard_map/all_to_all | solution.py:95
  404.3 384.5 %all-gather.7.cloned.1.call-start = ((), (), s32[]{:S(2)}) async-start(), calls=%async_computation.5 | async-start | bytes 9437184 | tf_op jit(solution)/shard_map/all_gather | solution.py:74
  673.9 2.4 copy-start.2
  883.9 127.4 %all-to-all-start.3 = ((bf16[5120,1,2,256]{3,2,1,0:T(2,128)(2,1)}), bf16[5120,1,2,256]{3,2,1,0:T(2,128)(2,1)}, u32[]{:S(2)}, u32[]{:S(2)}) async-start(bf16[5120,1,2,256]{3,2,1,0:T(2,128)(2,1)} %copy.73), calls=%async_computation.3 | async-start | bytes 10485760 | tf_op jit(solution)/shard_map/all_to_all | solution.py:110
Sparse Core Ops, SparseCore 0:
  171.0 110.6 all-gather.4
  680.3 108.3 all-gather.6
